TPU v7x, 128 devices: a whole 4x4x4 slice. The times are simulated.
128 devices in a mesh: row: 16 (over z, y_lo, core), col: 8 (over y_hi, x).
Axes of the slice: x: 4, y: 4 (y_hi: 2, y_lo: 2; y = y_hi * 2 + y_lo), z: 4, core: 2. Of those that a mesh axis runs over, the one named last changes fastest.
Arguments:
- panels: bfloat16 [1024, 32, 256], P(('row', 'col')), may hold values from -21 to 21
- tiles: bfloat16 [6144, 256, 512], P(('row', 'col')), may hold values from -0.109375 to 0.109375
- tile_dst: int32 [6144], P(('row', 'col')), may hold values from 0 to 7
- tile_src: int32 [6144], P(('row', 'col')), may hold values from 0 to 127
- geometry: float32 [1024, 6, 256], P(('row', 'col')), may hold values from -5 to 5
- areas: float32 [1024, 256], P(('row', 'col')), may hold values from 0.25 to 2
- block_owner: int32 [1024, 1], P(('row', 'col')), may hold values from 0 to 7; in each aligned block of 8 rows (0 to 7, 8 to 15, ...) at most 2 rows name the same one
- block_slot: int32 [1024], P(('row', 'col')), may hold values from 0 to 3
Outputs:
- field: float32 [1024, 32, 256], P(('row', 'col'))
- shape_gradient: float32 [1024, 256], P(('row', 'col'))
Inputs may be any that keep to these rules, and one draw needn't show every extreme that they name: Among the blocks of one device at most 2 have the same block_owner, and some device reaches 2.
All inputs are finite; a program needn't handle non-finite values.
Results may differ from a plain program's by a relative error of at most 0.0003.
Values may be sent and summed in bfloat16 or wider, within the bound.
A program may use at most 64 MiB of HBM per device.

v0:
```python
import jax
import jax.numpy as jnp
from jax import lax
from jax.sharding import PartitionSpec as P

CAP = 2
PD = 4


EPSILON = 1e-05


def make_basis(geometry, areas):
    normal = geometry[:, 0:3]
    place = geometry[:, 3:6]
    twist = jnp.stack(
        [
            place[:, 1] * normal[:, 2] - place[:, 2] * normal[:, 1],
            place[:, 2] * normal[:, 0] - place[:, 0] * normal[:, 2],
            place[:, 0] * normal[:, 1] - place[:, 1] * normal[:, 0],
        ],
        axis=1,
    )
    weight = areas[:, None, :]
    return jnp.concatenate([weight * normal, weight * twist, weight, weight], axis=1)


def split_complex(images, freq_count, node_count):
    real_part = images[:, :freq_count, :node_count] - images[:, freq_count:, node_count:]
    imag_part = images[:, :freq_count, node_count:] + images[:, freq_count:, :node_count]
    return jnp.concatenate([real_part, imag_part], axis=1)


def normalize(totals):
    return totals * lax.rsqrt(jnp.mean(totals * totals, axis=1, keepdims=True) + EPSILON)


def shards(panels, tiles, tile_dst, tile_src, geometry, areas, block_owner, block_slot):
    precise = lax.Precision.HIGHEST
    block_count, rows_twice, node_count = panels.shape
    freq_count = rows_twice // 2
    tile_count = tiles.shape[0]
    flat_panels = panels.reshape(block_count, rows_twice * node_count)
    gathered = lax.all_gather(flat_panels, "row", axis=0, tiled=True)
    count = gathered.shape[0]
    picking = (tile_src[:, None] == jnp.arange(count, dtype=jnp.int32)[None, :]).astype(
        jnp.bfloat16
    )
    picked = jnp.dot(picking, gathered, preferred_element_type=jnp.float32)
    chosen = picked.astype(jnp.bfloat16).reshape(tile_count, rows_twice, node_count)
    images = jnp.einsum("tjn,tnm->tjm", chosen, tiles, preferred_element_type=jnp.float32)
    tile_terms = split_complex(images, freq_count, node_count)
    target = (tile_dst[None, :] == jnp.arange(block_count, dtype=jnp.int32)[:, None]).astype(
        jnp.float32
    )
    near = jnp.einsum("dt,tjn->djn", target, tile_terms, precision=precise)
    incident = panels.astype(jnp.float32)
    field = 0.5 * incident + near
    power = field[:, :freq_count] ** 2 + field[:, freq_count:] ** 2
    cross_power = (
        incident[:, :freq_count] * field[:, :freq_count]
        + incident[:, freq_count:] * field[:, freq_count:]
    )
    basis = make_basis(geometry, areas)
    first_moments = jnp.einsum("bkn,bfn->bkf", basis[:, :7], power, precision=precise)
    last_moment = jnp.einsum("bn,bfn->bf", basis[:, 7], cross_power, precision=precise)
    moments = jnp.concatenate([first_moments, last_moment[:, None, :]], axis=1).reshape(
        block_count, -1
    )
    moment_width = moments.shape[1]
    group_count = lax.axis_size("col")
    owner = block_owner[:, 0]
    block_index = jnp.arange(block_count, dtype=jnp.int32)
    same_owner = owner[:, None] == owner[None, :]
    earlier = block_index[None, :] < block_index[:, None]
    rank = jnp.sum(jnp.where(same_owner & earlier, 1, 0), axis=1)
    slot_target = owner * CAP + rank
    slot_index = jnp.arange(group_count * CAP, dtype=jnp.int32)
    placing = slot_index[:, None] == slot_target[None, :]
    place_float = placing.astype(jnp.float32)
    send_values = jnp.dot(place_float, moments, precision=precise).reshape(
        group_count, CAP, moment_width
    )
    send_labels = (
        jnp.sum(jnp.where(placing, block_slot[None, :] + 1, 0), axis=1).astype(jnp.float32) - 1.0
    ).reshape(group_count, CAP)
    received, labels = (
        lax.all_to_all(send_values, "col", split_axis=0, concat_axis=0, tiled=True),
        lax.all_to_all(send_labels, "col", split_axis=0, concat_axis=0, tiled=True),
    )
    member = (
        labels.reshape(-1)[None, :] == jnp.arange(PD, dtype=jnp.int32).astype(jnp.float32)[:, None]
    ).astype(jnp.float32)
    totals = jnp.dot(member, received.reshape(-1, moment_width), precision=precise)
    adjoint = normalize(totals)
    answer = jnp.dot(member.T, adjoint, precision=precise).reshape(group_count, CAP, moment_width)
    returned = lax.all_to_all(answer, "col", split_axis=0, concat_axis=0, tiled=True)
    block_adjoint = jnp.dot(place_float.T, returned.reshape(-1, moment_width), precision=precise)
    shaped = block_adjoint.reshape(block_count, 8, freq_count)
    first_terms = jnp.einsum("bkf,bfn->bkn", shaped[:, :7], power, precision=precise)
    last_term = jnp.einsum("bf,bfn->bn", shaped[:, 7], cross_power, precision=precise)
    shape_gradient = (
        jnp.sum(basis[:, :7] * first_terms, axis=1) + basis[:, 7] * last_term
    ) / freq_count
    return (field, shape_gradient)


def solution(mesh):
    in_specs = (
        P(("row", "col"), None, None),
        P(("row", "col"), None, None),
        P(("row", "col")),
        P(("row", "col")),
        P(("row", "col"), None, None),
        P(("row", "col"), None),
        P(("row", "col"), None),
        P(("row", "col")),
    )
    out_specs = (P(("row", "col"), None, None), P(("row", "col"), None))
    return jax.shard_map(shards, mesh=mesh, in_specs=in_specs, out_specs=out_specs, check_vma=False)
```

profile of v0, /device:TPU:0, one launch (start us, length us, event | category | flops | bytes accessed | tf_op | source)
XLA Modules:
  0.0 94.8 jit_solution(7106194001397986972)
XLA Ops:
  7.2 1.6 %copy.87 = bf16[1,8,32,256]{3,1,2,0:T(8,128)(2,1)} copy(bf16[1,8,32,256]{3,2,1,0:T(8,128)(2,1)} %bitcast.44) | data formatting | bytes 262144
  8.9 0.9 select_reduce_fusion.1
  9.8 0.7 multiply_add_fusion.2
  10.6 0.7 sub.25
  11.2 7.0 %all-to-all-start = ((f32[8,1,2]{2,1,0:T(1,128)}), f32[8,1,2]{2,1,0:T(1,128)S(1)}, u32[]{:S(2)}, u32[]{:S(2)}) async-start(f32[8,1,2]{2,1,0:T(1,128)} %bitcast.3), calls=%async_computation | async-start | bytes 8192 | tf_op jit(solution)/shard_map/all_to_all | solution.py:89
  18.3 0.7 broadcast_in_dim.24
  19.0 0.7 slice.73
  19.7 0.8 fusion.42
  20.5 0.7 copy_multiply_fusion
  21.3 1.0 %copy_convert_fusion = f32[8,32,256]{2,0,1:T(8,128)S(1)} fusion(bf16[8,32,256]{2,1,0:T(8,128)(2,1)} %param.8), kind=kLoop, calls=%fused_computation.12 | loop fusion | flops 65536 | bytes 393216 | tf_op jit(solution)/shard_map/convert_element_type | solution.py:57
  22.3 24.3 %all-gather.2.cloned.1.call-done = bf16[128,8192]{1,0:T(8,128)(2,1)} async-done(((bf16[8,8192]{1,0:T(8,128)(2,1)}), bf16[128,8192]{1,0:T(8,128)(2,1)}) %all-gather.2.cloned.1.call-update) | async-done | bytes 2097168 | tf_op jit(solution)/shard_map/all_gather | solution.py:44
  46.6 2.1 %convolution_convert_fusion = bf16[48,8192]{1,0:T(8,128)(2,1)S(1)} fusion(bf16[128,8192]{1,0:T(8,128)(2,1)} %all-gather.2.cloned.1.call-done, s32[48]{0:T(128)} %param.11), kind=kOutput, calls=%fused_computation | convolution fusion | flops 101062656 | bytes 2883776 | tf_op jit(solution)/shard_map/dot_general | solution.py:49
  48.9 6.8 %fusion.43 = f32[48,32,512]{2,1,0:T(8,128)S(1)} fusion(bf16[48,32,256]{2,1,0:T(8,128)(2,1)S(1)} %bitcast.42, bf16[48,256,512]{2,1,0:T(8,128)(2,1)} %param.9), kind=kOutput, calls=%fused_computation.69 | convolution fusion | flops 402653184 | bytes 16515072 | tf_op jit(solution)/shard_map/tjn,tnm->tjm/dot_general | solution.py:51
  56.2 0.7 copy-done
  56.9 1.5 %fusion.2 = f32[8,32,256]{2,0,1:T(8,128)S(1)} fusion(f32[48,32,256]{2,1,0:T(8,128)S(1)} %pad_maximum_fusion, bf16[8,32,256]{2,1,0:T(8,128)(2,1)S(1)} %copy-done, s32[48]{0:T(128)S(1)} %copy-done.2), kind=kOutput, calls=%fused_computation.4 | convolution fusion | flops 37945728 | bytes 1966272 | tf_op jit(solution)/shard_map/dt,tjn->djn/dot_general | solution.py:56
  59.3 0.6 copy.70
  60.0 6.6 %all-to-all-start.1 = ((f32[8,2,128]{2,1,0:T(2,128)}), f32[8,2,128]{2,1,0:T(2,128)S(1)}, u32[]{:S(2)}, u32[]{:S(2)}) async-start(f32[8,2,128]{2,1,0:T(2,128)} %copy.70), calls=%async_computation.1 | async-start | bytes 16384 | tf_op jit(solution)/shard_map/all_to_all | solution.py:88
  67.0 0.7 reduce.3
  67.8 6.4 %all-to-all-done.1 = f32[8,2,128]{2,1,0:T(2,128)S(1)} async-done(((f32[8,2,128]{2,1,0:T(2,128)}), f32[8,2,128]{2,1,0:T(2,128)S(1)}, u32[]{:S(2)}, u32[]{:S(2)}) %all-to-all-start.1) | async-done | bytes 8224 | tf_op jit(solution)/shard_map/all_to_all | solution.py:88
  74.5 0.9 fusion.29
  75.4 3.3 %all-to-all-start.2 = ((f32[8,2,128]{2,1,0:T(2,128)}), f32[8,2,128]{2,1,0:T(2,128)S(1)}, u32[]{:S(2)}, u32[]{:S(2)}) async-start(f32[8,2,128]{2,1,0:T(2,128)} %bitcast.10), calls=%async_computation.2 | async-start | bytes 16384 | tf_op jit(solution)/shard_map/all_to_all | solution.py:97
  78.7 0.8 copy.74
  79.5 6.8 %all-to-all-done.2 = f32[8,2,128]{2,1,0:T(2,128)S(1)} async-done(((f32[8,2,128]{2,1,0:T(2,128)}), f32[8,2,128]{2,1,0:T(2,128)S(1)}, u32[]{:S(2)}, u32[]{:S(2)}) %all-to-all-start.2) | async-done | bytes 8224 | tf_op jit(solution)/shard_map/all_to_all | solution.py:97
  87.4 0.6 fusion.17
  (32 shorter events, 3.5 us)
Async XLA Ops:
  7.2 39.5 %all-gather.2.cloned.1.call-start = ((), (), s32[]{:S(2)}) async-start(), calls=%async_computation.3 | async-start | bytes 2228224 | tf_op jit(solution)/shard_map/all_gather | solution.py:44
  11.2 48.7 %all-to-all-start = ((f32[8,1,2]{2,1,0:T(1,128)}), f32[8,1,2]{2,1,0:T(1,128)S(1)}, u32[]{:S(2)}, u32[]{:S(2)}) async-start(f32[8,1,2]{2,1,0:T(1,128)} %bitcast.3), calls=%async_computation | async-start | bytes 8192 | tf_op jit(solution)/shard_map/all_to_all | solution.py:89
  56.0 0.9 copy-start
  56.0 0.9 copy-start.2
  56.9 1.6 %copy-start.1 = (f32[8,256]{1,0:T(8,128)S(1)}, f32[8,256]{1,0:T(8,128)}, u32[]{:S(2)}) copy-start(f32[8,256]{1,0:T(8,128)} %param.13) | copy-start | bytes 24580
  60.0 14.3 %all-to-all-start.1 = ((f32[8,2,128]{2,1,0:T(2,128)}), f32[8,2,128]{2,1,0:T(2,128)S(1)}, u32[]{:S(2)}, u32[]{:S(2)}) async-start(f32[8,2,128]{2,1,0:T(2,128)} %copy.70), calls=%async_computation.1 | async-start | bytes 16384 | tf_op jit(solution)/shard_map/all_to_all | solution.py:88
  75.4 11.0 %all-to-all-start.2 = ((f32[8,2,128]{2,1,0:T(2,128)}), f32[8,2,128]{2,1,0:T(2,128)S(1)}, u32[]{:S(2)}, u32[]{:S(2)}) async-start(f32[8,2,128]{2,1,0:T(2,128)} %bitcast.10), calls=%async_computation.2 | async-start | bytes 16384 | tf_op jit(solution)/shard_map/all_to_all | solution.py:97
Sparse Core Ops, SparseCore 0:
  10.2 36.3 all-gather.1
where the time goes:
time: 95.4 us; the launch traced here: 94.8 us
  waiting for transfers between devices  37.6 us (39%)
  starting transfers between devices  17 us (18%)
  between operations  14.2 us (15%)
  matrix products  13.1 us (14%)
  local copies, waits for them, and re-layouts  7.64 us (8%)
  other arithmetic  5.25 us (6%)
    all_gather x1, waiting for transfers between devices, shards(): gathered = lax.all_gather(flat_panels, 'row', axis=0, tiled=True)  24.3 us
    all_to_all x1, starting transfers between devices, shards(): lax.all_to_all(send_labels, 'col', split_axis=0, concat_axis=0, tiled=True)  7.04 us
    all_to_all x1, waiting for transfers between devices, shards(): lax.all_to_all(answer, 'col', split_axis=0, concat_axis=0, tiled=True)  6.84 us
    dot_general x1, matrix products, shards(): jnp.einsum('tjn,tnm->tjm', chosen, tiles, preferred_element_type=jnp.floa...  6.83 us
    all_to_all x1, starting transfers between devices, shards(): lax.all_to_all(send_values, 'col', split_axis=0, concat_axis=0, tiled=True)  6.56 us
    all_to_all x1, waiting for transfers between devices, shards(): lax.all_to_all(send_values, 'col', split_axis=0, concat_axis=0, tiled=True)  6.43 us
    unnamed x9, local copies, waits for them, and re-layouts  3.35 us
    all_to_all x1, starting transfers between devices, shards(): lax.all_to_all(answer, 'col', split_axis=0, concat_axis=0, tiled=True)  3.33 us
  transfers between devices with their start and end apart: 4, of which 3 were waited for; matrix products, arithmetic and copies ran while one was open for 22% of the time, Pallas kernels for 0%

commit v1 on v0

v1 whole, which is shorter than its diff:
```python
import functools

import jax
import jax.numpy as jnp
from jax import lax
from jax.experimental import pallas as pl
from jax.experimental.pallas import tpu as pltpu
from jax.sharding import PartitionSpec as P

MESH = pl.DeviceIdType.MESH
EPSILON = 1e-05
NBD = 8
TPD = 48
NF = 16
BN = 256
PD = 4
CYCLE = 128
GROUP = 8
CHUNK = 8
H = 4
MID0 = 2
MID1 = 6

UP, DOWN, SIDE = "up", "down", "side"
MOVES = (
    (UP, 0, 0, H, NBD, None),
    (DOWN, 0, 0, H, NBD, None),
    (SIDE, 0, 0, 0, H, None),
    (UP, 0, 0, 0, H, None),
    (DOWN, 0, 0, 0, H, None),
    (SIDE, 0, 0, H, NBD, None),
    (UP, -1, 0, H, MID1, 0),
    (DOWN, 1, 0, MID1, NBD, 1),
    (UP, 0, 1, 0, H, 2),
    (DOWN, 0, 1, 0, H, 2),
    (SIDE, -1, 0, H, NBD, 0),
    (SIDE, 1, 0, H, NBD, 1),
    (UP, -1, 0, 0, MID0, 3),
    (DOWN, 1, 0, MID0, H, 4),
    (SIDE, -2, 0, H, MID1, 6),
    (SIDE, 2, 0, MID1, NBD, 7),
    (UP, -1, 1, 0, MID0, 8),
    (DOWN, 1, 1, MID0, H, 9),
)
ORDER = tuple(range(len(MOVES)))


def split2(value):
    high = value.astype(jnp.bfloat16)
    low = (value - high.astype(jnp.float32)).astype(jnp.bfloat16)
    return high, low


def nt(left, right):
    return lax.dot_general(
        left, right, (((1,), (1,)), ((), ())), preferred_element_type=jnp.float32
    )


def kernel(
    panels,
    tiles,
    tile_dst,
    tile_src,
    geometry,
    areas,
    owner,
    slot,
    field_out,
    grad_out,
    gathered,
    tile_buf,
    left_re,
    left_im,
    acc,
    geo_buf,
    area_buf,
    field_buf,
    grad_buf,
    energy_high,
    energy_low,
    key_send,
    key_all,
    moment_send,
    moment_all,
    dst_smem,
    src_smem,
    owner_smem,
    slot_smem,
    load_sem,
    tile_sem,
    out_sem,
    send_sem,
    recv_sem,
    pair_send,
    pair_recv,
    key_send_sem,
    key_recv_sem,
    mom_send_sem,
    mom_recv_sem,
    wave_sem,
):
    row = lax.axis_index("row")
    col = lax.axis_index("col")
    z = row // 4
    y = lax.rem(row // 2, 2)
    core = lax.rem(row, 2)
    y_hi = col // 4
    x = lax.rem(col, 4)

    def row_of(dz, flip, other_core=0):
        zz = lax.rem(z + dz + 4, 4)
        yy = 1 - y if flip else y
        cc = 1 - core if other_core else core
        return zz * 4 + yy * 2 + cc

    up, down, side, pair = row_of(1, 0), row_of(-1, 0), row_of(0, 1), row_of(0, 0, 1)
    target = {UP: up, DOWN: down, SIDE: side}
    near = (
        {"row": row, "col": y_hi * 4 + lax.rem(x + 1, 4)},
        {"row": row, "col": y_hi * 4 + lax.rem(x + 3, 4)},
        {"row": side, "col": col},
        {"row": side, "col": (1 - y_hi) * 4 + x},
    )
    around = near + (
        {"row": up, "col": col},
        {"row": down, "col": col},
        {"row": pair, "col": col},
    )

    barrier = pltpu.get_barrier_semaphore()
    for device in around:
        pl.semaphore_signal(barrier, inc=1, device_id=device, device_id_type=MESH)

    loads = [
        pltpu.make_async_copy(
            panels, gathered.at[pl.ds(row * NBD, NBD)], load_sem.at[0]
        ),
        pltpu.make_async_copy(owner, owner_smem, load_sem.at[1]),
        pltpu.make_async_copy(slot, slot_smem, load_sem.at[2]),
        pltpu.make_async_copy(tile_dst, dst_smem, load_sem.at[3]),
        pltpu.make_async_copy(tile_src, src_smem, load_sem.at[4]),
        pltpu.make_async_copy(geometry, geo_buf, load_sem.at[5]),
        pltpu.make_async_copy(areas, area_buf, load_sem.at[6]),
    ]
    for load in loads:
        load.start()

    def region(dz, flip, first, end, other_core=0):
        return gathered.at[pl.ds(row_of(dz, flip, other_core) * NBD + first, end - first)]

    def move_copy(number):
        way, dz, flip, first, end, _ = MOVES[number]
        if dz == 0 and flip == 0:
            source = panels.at[pl.ds(first, end - first)]
        else:
            source = region(dz, flip, first, end)
        return pltpu.make_async_remote_copy(
            src_ref=source,
            dst_ref=region(dz, flip, first, end),
            send_sem=send_sem.at[number],
            recv_sem=recv_sem.at[number],
            device_id={"row": target[way]},
            device_id_type=MESH,
        )

    def landed(number):
        way, dz, flip, first, end, _ = MOVES[number]
        if way == UP:
            return dz - 1, flip, first, end
        if way == DOWN:
            return dz + 1, flip, first, end
        return dz, 1 - flip, first, end

    def pair_copy(number):
        if number < 0:
            source, where, slot_number = panels, (0, 0, 0, NBD), len(MOVES)
            destination = region(*where)
        else:
            source = destination = region(*landed(number))
            slot_number = number
        return pltpu.make_async_remote_copy(
            src_ref=source,
            dst_ref=destination,
            send_sem=pair_send.at[slot_number],
            recv_sem=pair_recv.at[slot_number],
            device_id={"row": pair},
            device_id_type=MESH,
        )

    tile_loads = [
        pltpu.make_async_copy(
            tiles.at[pl.ds(step * CHUNK, CHUNK)],
            tile_buf.at[pl.ds(step * CHUNK, CHUNK)],
            tile_sem.at[step],
        )
        for step in range(TPD // CHUNK)
    ]

    pl.semaphore_wait(barrier, len(around))

    for number, move in enumerate(MOVES):
        if move[5] is None:
            move_copy(number).start()
    pair_copy(-1).start()
    for load in tile_loads:
        load.start()

    def wave_signal(number):
        for device in near:
            pl.semaphore_signal(
                wave_sem.at[number], inc=1, device_id=device, device_id_type=MESH
            )

    wave_signal(0)

    def arrive(number):
        move_copy(number).wait_recv()
        for later, move in enumerate(MOVES):
            if move[5] == number:
                move_copy(later).start()
        pair_copy(number).start()

    lane = lax.broadcasted_iota(jnp.int32, (1, 128), 1)
    lane_block = lane // NF

    def key_copy(step):
        return pltpu.make_async_remote_copy(
            src_ref=key_send,
            dst_ref=key_all.at[pl.ds(step * 8, 8)],
            send_sem=key_send_sem.at[step],
            recv_sem=key_recv_sem.at[step],
            device_id={"col": lax.rem(col + step, GROUP)},
            device_id_type=MESH,
        )

    def moment_copy(step):
        return pltpu.make_async_remote_copy(
            src_ref=moment_send,
            dst_ref=moment_all.at[pl.ds(step * 8, 8)],
            send_sem=mom_send_sem.at[step],
            recv_sem=mom_recv_sem.at[step],
            device_id={"col": lax.rem(col + step, GROUP)},
            device_id_type=MESH,
        )

    loads[1].wait()
    loads[2].wait()
    keys = [owner_smem[b] * PD + slot_smem[b] for b in range(NBD)]
    key_lane = jnp.zeros((8, 128), jnp.int32)
    for b in range(NBD):
        key_lane = jnp.where(lane_block == b, keys[b], key_lane)
    key_send[...] = key_lane
    key_all[pl.ds(0, 8), :] = key_lane

    wave_at = {2: 0, 5: 1, 8: 2}
    for place, number in enumerate(ORDER):
        arrive(number)
        if place in wave_at:
            wave = wave_at[place]
            pl.semaphore_wait(wave_sem.at[wave], len(near))
            if wave < 2:
                wave_signal(wave + 1)
            else:
                for step in range(1, GROUP):
                    key_copy(step).start()

    loads[5].wait()
    loads[6].wait()
    weight = area_buf[...]
    n0, n1, n2 = geo_buf[0], geo_buf[1], geo_buf[2]
    p0, p1, p2 = geo_buf[3], geo_buf[4], geo_buf[5]
    basis = jnp.concatenate(
        [
            weight * n0,
            weight * n1,
            weight * n2,
            weight * (p1 * n2 - p2 * n1),
            weight * (p2 * n0 - p0 * n2),
            weight * (p0 * n1 - p1 * n0),
            weight,
            weight,
        ],
        axis=0,
    )
    basis_high, basis_low = split2(basis)

    for load in loads[3:5]:
        load.wait()
    loads[0].wait()
    for load in tile_loads:
        load.wait()
    acc[...] = jnp.zeros_like(acc)
    pair_copy(-1).wait_recv()
    for number in ORDER:
        pair_copy(number).wait_recv()

    def step_body(step, carry):
        for inner in range(CHUNK):
            number = step * CHUNK + inner
            panel = gathered[src_smem[number]]
            turned = jnp.concatenate([-panel[NF:], panel[:NF]], axis=0)
            place = dst_smem[number]
            for d in range(NBD):
                keep = jnp.where(place == d, 1.0, 0.0).astype(jnp.float32)
                keep = jnp.full((2 * NF, BN), keep, jnp.float32).astype(jnp.bfloat16)
                rows = pl.ds(d * 2 * NF, 2 * NF)
                columns = pl.ds(inner * BN, BN)
                left_re[rows, columns] = panel * keep
                left_im[rows, columns] = turned * keep
        block = tile_buf[pl.ds(step * CHUNK, CHUNK)]
        real = block[:, :, :BN].reshape(CHUNK * BN, BN)
        imag = block[:, :, BN:].reshape(CHUNK * BN, BN)
        acc[...] += jnp.dot(
            left_re[...], real, preferred_element_type=jnp.float32
        ) + jnp.dot(left_im[...], imag, preferred_element_type=jnp.float32)
        return carry

    lax.fori_loop(0, TPD // CHUNK, step_body, 0)

    for b in range(NBD):
        incident = gathered[row * NBD + b].astype(jnp.float32)
        field = 0.5 * incident + acc[pl.ds(b * 2 * NF, 2 * NF), :]
        field_buf[b] = field
        re, im = field[:NF], field[NF:]
        high, low = split2(re * re + im * im)
        energy_high[pl.ds(b * NF, NF), :] = high
        energy_low[pl.ds(b * NF, NF), :] = low
        high, low = split2(incident[:NF] * re + incident[NF:] * im)
        energy_high[pl.ds(128 + b * NF, NF), :] = high
        energy_low[pl.ds(128 + b * NF, NF), :] = low

    field_copy = pltpu.make_async_copy(field_buf, field_out, out_sem.at[0])
    field_copy.start()

    high = energy_high[...]
    low = energy_low[...]
    products = nt(basis_high, high) + nt(basis_high, low) + nt(basis_low, high)
    own = lax.broadcasted_iota(jnp.int32, (8, 128), 0) == lane_block
    row_index = lax.broadcasted_iota(jnp.int32, (8, 128), 0)
    moments = jnp.zeros((8, 128), jnp.float32)
    for k in range(8):
        side_columns = slice(0, 128) if k < 7 else slice(128, 256)
        part = jnp.where(own, products[k * 8 : k * 8 + 8, side_columns], 0.0)
        total = jnp.sum(part, axis=0, keepdims=True)
        moments = jnp.where(row_index == k, total, moments)
    moment_send[...] = moments
    moment_all[pl.ds(0, 8), :] = moments
    for step in range(1, GROUP):
        moment_copy(step).start()

    for step in range(1, GROUP):
        key_copy(step).wait_recv()
    matches = []
    key_rows = [key_all[c * 8 : c * 8 + 1, :] for c in range(GROUP)]
    same_f = lax.broadcasted_iota(jnp.int32, (NF, 128), 0) == lax.rem(
        lax.broadcasted_iota(jnp.int32, (NF, 128), 1), NF
    )
    columns = []
    for c in range(GROUP):
        pieces = []
        for b in range(NBD):
            pieces.append(
                jnp.where(
                    jnp.logical_and(key_rows[c] == keys[b], same_f), 1.0, 0.0
                ).astype(jnp.bfloat16)
            )
        columns.append(jnp.concatenate(pieces, axis=0))

    totals = jnp.zeros((16, 128), jnp.float32)
    for c in range(GROUP):
        if c:
            moment_copy(c).wait_recv()
        high_part, low_part = split2(moment_all[c * 8 : c * 8 + 8, :])
        totals = totals + nt(jnp.concatenate([high_part, low_part], axis=0), columns[c])
    totals = totals[:8] + totals[8:]

    squares = jnp.zeros((8, 128), jnp.float32)
    lefts = []
    for k in range(8):
        spread = jnp.where(own, totals[k : k + 1, :], 0.0)
        squares = squares + spread * spread
        none = jnp.zeros_like(spread)
        lefts.append(jnp.concatenate([spread, none] if k < 7 else [none, spread], axis=1))
    left_high, left_low = split2(jnp.concatenate(lefts, axis=0))
    scale = lax.rsqrt(jnp.sum(squares, axis=1, keepdims=True) * (1.0 / 128) + EPSILON)
    dot = functools.partial(jnp.dot, preferred_element_type=jnp.float32)
    terms = (dot(left_high, high) + dot(left_high, low) + dot(left_low, high)) * basis
    gradient = terms[0:8]
    for k in range(1, 8):
        gradient = gradient + terms[k * 8 : k * 8 + 8]
    grad_buf[...] = gradient * (scale * (1.0 / NF))
    grad_copy = pltpu.make_async_copy(grad_buf, grad_out, out_sem.at[1])
    grad_copy.start()

    for number in range(len(MOVES)):
        move_copy(number).wait_send()
        pair_copy(number).wait_send()
    pair_copy(-1).wait_send()
    for step in range(1, GROUP):
        key_copy(step).wait_send()
        moment_copy(step).wait_send()
    field_copy.wait()
    grad_copy.wait()


def shards(panels, tiles, tile_dst, tile_src, geometry, areas, block_owner, block_slot):
    anywhere = pl.BlockSpec(memory_space=pl.ANY)
    count = len(MOVES)
    dma = pltpu.SemaphoreType.DMA
    return pl.pallas_call(
        kernel,
        out_shape=(
            jax.ShapeDtypeStruct((NBD, 2 * NF, BN), jnp.float32),
            jax.ShapeDtypeStruct((NBD, BN), jnp.float32),
        ),
        in_specs=[anywhere] * 8,
        out_specs=(anywhere, anywhere),
        scratch_shapes=[
            pltpu.VMEM((CYCLE, 2 * NF, BN), jnp.bfloat16),
            pltpu.VMEM((TPD, BN, 2 * BN), jnp.bfloat16),
            pltpu.VMEM((NBD * 2 * NF, CHUNK * BN), jnp.bfloat16),
            pltpu.VMEM((NBD * 2 * NF, CHUNK * BN), jnp.bfloat16),
            pltpu.VMEM((NBD * 2 * NF, BN), jnp.float32),
            pltpu.VMEM((6, NBD, BN), jnp.float32),
            pltpu.VMEM((NBD, BN), jnp.float32),
            pltpu.VMEM((NBD, 2 * NF, BN), jnp.float32),
            pltpu.VMEM((NBD, BN), jnp.float32),
            pltpu.VMEM((2 * NBD * NF, BN), jnp.bfloat16),
            pltpu.VMEM((2 * NBD * NF, BN), jnp.bfloat16),
            pltpu.VMEM((8, 128), jnp.int32),
            pltpu.VMEM((GROUP * 8, 128), jnp.int32),
            pltpu.VMEM((8, 128), jnp.float32),
            pltpu.VMEM((GROUP * 8, 128), jnp.float32),
            pltpu.SMEM((TPD,), jnp.int32),
            pltpu.SMEM((TPD,), jnp.int32),
            pltpu.SMEM((NBD,), jnp.int32),
            pltpu.SMEM((NBD,), jnp.int32),
            dma((7,)),
            dma((TPD // CHUNK,)),
            dma((2,)),
            dma((count,)),
            dma((count,)),
            dma((count + 1,)),
            dma((count + 1,)),
            dma((GROUP,)),
            dma((GROUP,)),
            dma((GROUP,)),
            dma((GROUP,)),
            pltpu.SemaphoreType.REGULAR((3,)),
        ],
        compiler_params=pltpu.CompilerParams(collective_id=0, has_side_effects=True),
    )(
        panels,
        tiles,
        tile_dst,
        tile_src,
        jnp.transpose(geometry, (1, 0, 2)),
        areas,
        block_owner.reshape(-1),
        block_slot,
    )


def solution(mesh):
    in_specs = (
        P(("row", "col"), None, None),
        P(("row", "col"), None, None),
        P(("row", "col")),
        P(("row", "col")),
        P(("row", "col"), None, None),
        P(("row", "col"), None),
        P(("row", "col"), None),
        P(("row", "col")),
    )
    out_specs = (P(("row", "col"), None, None), P(("row", "col"), None))
    return jax.shard_map(shards, mesh=mesh, in_specs=in_specs, out_specs=out_specs, check_vma=False)
```

time: 95.4 us -> 34.5 us (0.36)
  the two profiles are of different devices: /device:TPU:0 before, /device:TPU:1 now
where the time goes in v1:
time: 34.5 us; the launch traced here: 34.3 us
  Pallas kernels  30.7 us (89%)
  local copies, waits for them, and re-layouts  2.97 us (9%)
  between operations  0.64 us (2%)
    pallas_call x1, Pallas kernels, shards(): pl.pallas_call(kernel, out_shape=(jax.ShapeDtypeStruct((NBD, 2 * NF, BN),...  30.7 us
    unnamed x2, local copies, waits for them, and re-layouts  2.97 us

profile of v1, /device:TPU:1, one launch (start us, length us, event | category | flops | bytes accessed | tf_op | source)
XLA Modules:
  0.0 34.3 jit_solution(10003047618271512975)
XLA Ops:
  0.6 30.7 %shard_map.95 = (f32[8,32,256]{2,1,0:T(8,128)}, f32[8,256]{1,0:T(8,128)}) custom-call(bf16[8,32,256]{2,1,0:T(8,128)(2,1)} %panels.1, bf16[48,256,512]{2,1,0:T(8,128)(2,1)} %tiles.1, s32[48]{0:T(128)} %tile_dst.1, s32[48]{0:T(128)} %tile_src.1, f32[6,8,256]{2,1,0:T(8,128)} %bitcast.2, f32[8,256]{1,0:T(8,128)} %areas.1, s32[8]{0:T(128)} %bitcast.3, s32[8]{0:T(128)} %slot.1), custom_call_target="tpu_custom_call" | custom-call | tf_op jit(solution)/shard_map/pallas_call | solution.py:411
  31.3 1.7 %copy.12 = f32[8,32,256]{2,1,0:T(8,128)} copy(f32[8,32,256]{2,1,0:T(8,128)} %get-tuple-element.4) | data formatting | bytes 524288
  33.0 1.3 %copy.13 = f32[8,256]{1,0:T(8,128)} copy(f32[8,256]{1,0:T(8,128)} %get-tuple-element.5) | data formatting | bytes 16384

commit v2 on v0

v2 whole, which is shorter than its diff:
```python
import functools

import jax
import jax.numpy as jnp
from jax import lax
from jax.experimental import pallas as pl
from jax.experimental.pallas import tpu as pltpu
from jax.sharding import PartitionSpec as P

MESH = pl.DeviceIdType.MESH
EPSILON = 1e-05
NBD = 8
TPD = 48
NF = 16
BN = 256
PD = 4
CYCLE = 128
GROUP = 8
CHUNK = 24
UNIT = 2
HALF = 128
ACROSS = 4
LAG = 8
UP, DOWN, SIDE = "up", "down", "side"


def plan_rounds():
    sends = {}

    def add(send, source, hops):
        sends[send] = (source, 2 * hops + (send[4] == 0))

    for half in range(2):
        for b in range(0, NBD, UNIT):
            upward = b % 4 < 2
            two = UP if upward else DOWN
            near, far = (-1, -2) if upward else (1, 2)
            if b < ACROSS:
                first = (SIDE, 0, 0, b, half)
                add(first, None, 2)
                for link in (UP, DOWN):
                    add((link, 0, 0, b, half), None, int(link == two))
                    add((link, 0, 1, b, half), first, int(link == two))
                add((two, near, 0, b, half), (two, 0, 0, b, half), 0)
                add((two, near, 1, b, half), (two, 0, 1, b, half), 0)
            else:
                add((SIDE, 0, 0, b, half), None, 0)
                add((UP, 0, 0, b, half), None, 2 if upward else 1)
                add((DOWN, 0, 0, b, half), None, 1 if upward else 2)
                add((SIDE, -1, 0, b, half), (UP, 0, 0, b, half), 0)
                add((SIDE, 1, 0, b, half), (DOWN, 0, 0, b, half), 0)
                add((two, near, 0, b, half), (two, 0, 0, b, half), 1)
                add((SIDE, far, 0, b, half), (two, near, 0, b, half), 0)
    left, sent, rounds = dict(sends), {}, []
    while left:
        now = []
        for link in (UP, DOWN, SIDE):
            ready = [
                send
                for send in left
                if send[0] == link
                and (left[send][0] is None or sent.get(left[send][0], len(rounds)) + LAG <= len(rounds))
            ]
            if ready:
                now.append(max(ready, key=lambda one: (left[one][1], left[one][0] is not None)))
        for send in now:
            sent[send] = len(rounds)
            del left[send]
        rounds.append(now)
    return rounds


ROUNDS = plan_rounds()
SENT = sum(len(sends) for sends in ROUNDS) // 2
WAVES = {LAG + 5: 0, LAG + 10: 1, LAG + 15: 2}


def split2(value):
    high = value.astype(jnp.bfloat16)
    low = (value - high.astype(jnp.float32)).astype(jnp.bfloat16)
    return high, low


def nt(left, right):
    return lax.dot_general(
        left, right, (((1,), (1,)), ((), ())), preferred_element_type=jnp.float32
    )


def kernel(
    panels,
    tiles,
    tile_dst,
    tile_src,
    geometry,
    areas,
    owner,
    slot,
    field_out,
    grad_out,
    first_half,
    second_half,
    images,
    tile_buf,
    acc,
    geo_buf,
    key_send,
    key_all,
    moment_send,
    moment_all,
    tile_smem,
    block_smem,
    load_sem,
    round_sem,
    pair_sem,
    copy_sem,
    wave_sem,
):
    row = lax.axis_index("row")
    col = lax.axis_index("col")
    z = row // 4
    y = lax.rem(row // 2, 2)
    core = lax.rem(row, 2)
    y_hi = col // 4
    x = lax.rem(col, 4)

    def row_of(dz, flip, other_core=0):
        zz = lax.rem(z + dz + 4, 4)
        yy = 1 - y if flip else y
        cc = 1 - core if other_core else core
        return zz * 4 + yy * 2 + cc

    up, down, side, pair = row_of(1, 0), row_of(-1, 0), row_of(0, 1), row_of(0, 0, 1)
    target = {UP: up, DOWN: down, SIDE: side}
    near = (
        {"row": row, "col": y_hi * 4 + lax.rem(x + 1, 4)},
        {"row": row, "col": y_hi * 4 + lax.rem(x + 3, 4)},
        {"row": side, "col": col},
        {"row": side, "col": (1 - y_hi) * 4 + x},
    )
    around = near + (
        {"row": up, "col": col},
        {"row": down, "col": col},
        {"row": pair, "col": col},
    )

    barrier = pltpu.get_barrier_semaphore()
    for device in around:
        pl.semaphore_signal(barrier, inc=1, device_id=device, device_id_type=MESH)

    halves = (first_half, second_half)
    for half in range(2):
        pltpu.make_async_copy(
            panels.at[:, :, pl.ds(half * HALF, HALF)],
            halves[half].at[pl.ds(row * NBD, NBD)],
            load_sem.at[0],
        ).start()
    for place, source in enumerate((owner, slot)):
        pltpu.make_async_copy(source, block_smem.at[place], load_sem.at[1]).start()
    for place, source in enumerate((tile_dst, tile_src)):
        pltpu.make_async_copy(source, tile_smem.at[place], load_sem.at[2]).start()
    pltpu.make_async_copy(geometry, geo_buf.at[pl.ds(0, 6)], load_sem.at[3]).start()
    pltpu.make_async_copy(areas, geo_buf.at[6], load_sem.at[3]).start()

    def take(ref, sem):
        pltpu.make_async_copy(ref, ref, sem).wait()

    def blocks(half, dz, flip, b, count):
        return halves[half].at[pl.ds(row_of(dz, flip) * NBD + b, count)]

    def send(number, link, dz, flip, b, half):
        where = blocks(half, dz, flip, b, UNIT)
        pltpu.make_async_remote_copy(
            src_ref=where,
            dst_ref=where,
            send_sem=copy_sem.at[0],
            recv_sem=round_sem.at[number],
            device_id={"row": target[link]},
            device_id_type=MESH,
        ).start()

    def share(half, where):
        pltpu.make_async_remote_copy(
            src_ref=where,
            dst_ref=where,
            send_sem=copy_sem.at[1],
            recv_sem=pair_sem.at[half],
            device_id={"row": pair},
            device_id_type=MESH,
        ).start()

    def to_peers(source, destination, send_sem, recv_sem):
        for step in range(1, GROUP):
            pltpu.make_async_remote_copy(
                src_ref=source,
                dst_ref=destination.at[pl.ds(step * 8, 8)],
                send_sem=send_sem,
                recv_sem=recv_sem,
                device_id={"col": lax.rem(col + step, GROUP)},
                device_id_type=MESH,
            ).start()

    def greet(number):
        for device in near:
            pl.semaphore_signal(
                wave_sem.at[number], inc=1, device_id=device, device_id_type=MESH
            )

    take(first_half.at[pl.ds(0, 2 * NBD)], load_sem.at[0])
    pl.semaphore_wait(barrier, len(around))

    for number in range(LAG):
        for one in ROUNDS[number]:
            send(number, *one)
    for half in range(2):
        share(half, blocks(half, 0, 0, 0, NBD))
    for step in range(4):
        part = pl.ds(step * (TPD // 4), TPD // 4)
        pltpu.make_async_copy(tiles.at[part], tile_buf.at[part], load_sem.at[4]).start()
    greet(0)

    take(block_smem, load_sem.at[1])
    lane_block = lax.broadcasted_iota(jnp.int32, (8, 128), 1) // NF
    keys = [block_smem[0, b] * PD + block_smem[1, b] for b in range(NBD)]
    key_lane = jnp.zeros((8, 128), jnp.int32)
    for b in range(NBD):
        key_lane = jnp.where(lane_block == b, keys[b], key_lane)
    key_send[...] = key_lane
    key_all[pl.ds(0, 8), :] = key_lane

    for number in range(LAG, len(ROUNDS) + LAG):
        landed = ROUNDS[number - LAG]
        take(first_half.at[pl.ds(0, UNIT * len(landed))], round_sem.at[number - LAG])
        if number < len(ROUNDS):
            for one in ROUNDS[number]:
                send(number, *one)
        for link, dz, flip, b, half in landed:
            if link == SIDE:
                share(half, blocks(half, dz, 1 - flip, b, UNIT))
            else:
                share(half, blocks(half, dz + (1 if link == DOWN else -1), flip, b, UNIT))
        if number in WAVES:
            wave = WAVES[number]
            pl.semaphore_wait(wave_sem.at[wave], len(near))
            if wave < 2:
                greet(wave + 1)
            else:
                to_peers(key_send, key_all, copy_sem.at[3], copy_sem.at[4])

    take(geo_buf, load_sem.at[3])
    weight = geo_buf[6]
    n0, n1, n2 = geo_buf[0], geo_buf[1], geo_buf[2]
    p0, p1, p2 = geo_buf[3], geo_buf[4], geo_buf[5]
    basis = jnp.concatenate(
        [
            weight * n0,
            weight * n1,
            weight * n2,
            weight * (p1 * n2 - p2 * n1),
            weight * (p2 * n0 - p0 * n2),
            weight * (p0 * n1 - p1 * n0),
            weight,
            weight,
        ],
        axis=0,
    )
    basis_high, basis_low = split2(basis)

    take(tile_smem, load_sem.at[2])
    take(tile_buf, load_sem.at[4])
    acc[...] = jnp.zeros_like(acc)
    everything = pl.ds(0, UNIT * SENT + NBD)

    dot = functools.partial(jnp.dot, preferred_element_type=jnp.float32)

    def image_of(half, number):
        panel = halves[half][tile_smem[1, number]]
        turned = jnp.concatenate([-panel[NF:], panel[:NF]], axis=0)
        nodes = pl.ds(half * HALF, HALF)
        tile = jnp.concatenate(
            [tile_buf[number, nodes, pl.ds(0, BN)], tile_buf[number, nodes, pl.ds(BN, BN)]], axis=0
        )
        return dot(jnp.concatenate([panel, turned], axis=1), tile)

    def first_step(step, carry):
        for inner in range(CHUNK):
            number = step * CHUNK + inner
            images[number] = image_of(0, number)
        return carry

    def second_step(step, carry):
        for inner in range(CHUNK):
            number = step * CHUNK + inner
            image = images[number] + image_of(1, number)
            place = tile_smem[0, number]
            for d in range(NBD):
                acc[d] += jnp.where(place == d, 1.0, 0.0) * image
        return carry

    take(first_half.at[everything], pair_sem.at[0])
    lax.fori_loop(0, TPD // CHUNK, first_step, 0)
    take(second_half.at[everything], pair_sem.at[1])
    lax.fori_loop(0, TPD // CHUNK, second_step, 0)

    energies = ([], [], [], [])
    for b in range(NBD):
        incident = jnp.concatenate([part[row * NBD + b] for part in halves], axis=1).astype(jnp.float32)
        field = 0.5 * incident + acc[b]
        field_out[b] = field
        re, im = field[:NF], field[NF:]
        for place, value in enumerate((re * re + im * im, incident[:NF] * re + incident[NF:] * im)):
            first, second = split2(value)
            energies[place].append(first)
            energies[2 + place].append(second)
    high = jnp.concatenate(energies[0] + energies[1], axis=0)
    low = jnp.concatenate(energies[2] + energies[3], axis=0)
    products = nt(basis_high, high) + nt(basis_high, low) + nt(basis_low, high)
    row_index = lax.broadcasted_iota(jnp.int32, (8, 128), 0)
    own = row_index == lane_block
    moments = jnp.zeros((8, 128), jnp.float32)
    for k in range(8):
        side_columns = slice(0, 128) if k < 7 else slice(128, 256)
        part = jnp.where(own, products[k * 8 : k * 8 + 8, side_columns], 0.0)
        total = jnp.sum(part, axis=0, keepdims=True)
        moments = jnp.where(row_index == k, total, moments)
    moment_send[...] = moments
    moment_all[pl.ds(0, 8), :] = moments
    to_peers(moment_send, moment_all, copy_sem.at[5], copy_sem.at[6])

    take(key_all.at[pl.ds(8, 56)], copy_sem.at[4])
    same_f = lax.broadcasted_iota(jnp.int32, (NF, 128), 0) == lax.rem(
        lax.broadcasted_iota(jnp.int32, (NF, 128), 1), NF
    )
    columns = []
    for c in range(GROUP):
        key_row = key_all[c * 8 : c * 8 + 1, :]
        pieces = [
            jnp.where(jnp.logical_and(key_row == keys[b], same_f), 1.0, 0.0).astype(jnp.bfloat16)
            for b in range(NBD)
        ]
        columns.append(jnp.concatenate(pieces, axis=0))
    match = jnp.concatenate(columns, axis=1)

    take(moment_all.at[pl.ds(8, 56)], copy_sem.at[6])
    everyone = jnp.concatenate([moment_all[c * 8 : c * 8 + 8, :] for c in range(GROUP)], axis=1)
    totals = nt(jnp.concatenate(split2(everyone), axis=0), match)
    totals = totals[:8] + totals[8:]

    squares = jnp.zeros((8, 128), jnp.float32)
    lefts = []
    for k in range(8):
        spread = jnp.where(own, totals[k : k + 1, :], 0.0)
        squares = squares + spread * spread
        none = jnp.zeros_like(spread)
        lefts.append(jnp.concatenate([spread, none] if k < 7 else [none, spread], axis=1))
    left_high, left_low = split2(jnp.concatenate(lefts, axis=0))
    scale = lax.rsqrt(jnp.sum(squares, axis=1, keepdims=True) * (1.0 / 128) + EPSILON)
    terms = (dot(left_high, high) + dot(left_high, low) + dot(left_low, high)) * basis
    gradient = terms[0:8]
    for k in range(1, 8):
        gradient = gradient + terms[k * 8 : k * 8 + 8]
    grad_out[...] = gradient * (scale * (1.0 / NF))

    take(first_half.at[pl.ds(0, 2 * UNIT * SENT)], copy_sem.at[0])
    take(first_half.at[pl.ds(0, 2 * (UNIT * SENT + NBD))], copy_sem.at[1])
    take(key_all.at[pl.ds(8, 56)], copy_sem.at[3])
    take(moment_all.at[pl.ds(8, 56)], copy_sem.at[5])


def store(field, gradient, field_out, grad_out, sem):
    copies = [
        pltpu.make_async_copy(field, field_out, sem.at[0]),
        pltpu.make_async_copy(gradient, grad_out, sem.at[1]),
    ]
    for copy in copies:
        copy.start()
    for copy in copies:
        copy.wait()


def shards(panels, tiles, tile_dst, tile_src, geometry, areas, block_owner, block_slot):
    anywhere = pl.BlockSpec(memory_space=pl.ANY)
    vmem = pl.BlockSpec(memory_space=pltpu.VMEM)
    dma = pltpu.SemaphoreType.DMA
    field_shape = (NBD, 2 * NF, BN)
    grad_shape = (NBD, BN)
    field, gradient = pl.pallas_call(
        kernel,
        out_shape=(pltpu.VMEM(field_shape, jnp.float32), pltpu.VMEM(grad_shape, jnp.float32)),
        in_specs=[anywhere] * 8,
        out_specs=(vmem, vmem),
        scratch_shapes=[
            pltpu.VMEM((CYCLE, 2 * NF, HALF), jnp.bfloat16),
            pltpu.VMEM((CYCLE, 2 * NF, HALF), jnp.bfloat16),
            pltpu.VMEM((TPD, 2 * NF, BN), jnp.float32),
            pltpu.VMEM((TPD, BN, 2 * BN), jnp.bfloat16),
            pltpu.VMEM((NBD, 2 * NF, BN), jnp.float32),
            pltpu.VMEM((7, NBD, BN), jnp.float32),
            pltpu.VMEM((8, 128), jnp.int32),
            pltpu.VMEM((GROUP * 8, 128), jnp.int32),
            pltpu.VMEM((8, 128), jnp.float32),
            pltpu.VMEM((GROUP * 8, 128), jnp.float32),
            pltpu.SMEM((2, TPD), jnp.int32),
            pltpu.SMEM((2, NBD), jnp.int32),
            dma((5,)),
            dma((len(ROUNDS),)),
            dma((2,)),
            dma((7,)),
            pltpu.SemaphoreType.REGULAR((3,)),
        ],
        compiler_params=pltpu.CompilerParams(collective_id=0, has_side_effects=True),
    )(
        panels,
        tiles,
        tile_dst,
        tile_src,
        jnp.transpose(geometry, (1, 0, 2)),
        areas,
        block_owner.reshape(-1),
        block_slot,
    )
    return pl.pallas_call(
        store,
        out_shape=(
            jax.ShapeDtypeStruct(field_shape, jnp.float32),
            jax.ShapeDtypeStruct(grad_shape, jnp.float32),
        ),
        in_specs=[vmem, vmem],
        out_specs=(anywhere, anywhere),
        scratch_shapes=[dma((2,))],
    )(
        pltpu.with_memory_space_constraint(field, pltpu.VMEM),
        pltpu.with_memory_space_constraint(gradient, pltpu.VMEM),
    )


def solution(mesh):
    in_specs = (
        P(("row", "col"), None, None),
        P(("row", "col"), None, None),
        P(("row", "col")),
        P(("row", "col")),
        P(("row", "col"), None, None),
        P(("row", "col"), None),
        P(("row", "col"), None),
        P(("row", "col")),
    )
    out_specs = (P(("row", "col"), None, None), P(("row", "col"), None))
    return jax.shard_map(shards, mesh=mesh, in_specs=in_specs, out_specs=out_specs, check_vma=False)
```

time: 95.4 us -> 28.8 us (0.30)
  the two profiles are of different devices: /device:TPU:0 before, /device:TPU:1 now
where the time goes in v2:
time: 28.8 us; the launch traced here: 28.7 us
  Pallas kernels  28 us (97%)
  between operations  0.64 us (2%)
    pallas_call x1, Pallas kernels, shards(): pl.pallas_call(kernel, out_shape=(pltpu.VMEM(field_shape, jnp.float32), p...  27.3 us
    pallas_call x1, Pallas kernels, shards(): pl.pallas_call(store, out_shape=(jax.ShapeDtypeStruct(field_shape, jnp.fl...  0.72 us

profile of v2, /device:TPU:1, one launch (start us, length us, event | category | flops | bytes accessed | tf_op | source)
XLA Modules:
  0.0 28.7 jit_solution(15331852488762667927)
XLA Ops:
  0.6 27.3 %shard_map.95 = (f32[8,32,256]{2,1,0:T(8,128)S(1)}, f32[8,256]{1,0:T(8,128)S(1)}) custom-call(bf16[8,32,256]{2,1,0:T(8,128)(2,1)} %panels.1, bf16[48,256,512]{2,1,0:T(8,128)(2,1)} %tiles.1, s32[48]{0:T(128)} %tile_dst.1, s32[48]{0:T(128)} %tile_src.1, f32[6,8,256]{2,1,0:T(8,128)} %bitcast.2, f32[8,256]{1,0:T(8,128)} %areas.1, s32[8]{0:T(128)} %bitcast.3, s32[8]{0:T(128)} %slot.1), custom_call_target="tpu_custom_call" | custom-call | tf_op jit(solution)/shard_map/pallas_call | solution.py:387
  27.9 0.7 %shard_map.96 = (f32[8,32,256]{2,1,0:T(8,128)}, f32[8,256]{1,0:T(8,128)}) custom-call(f32[8,32,256]{2,1,0:T(8,128)S(1)} %get-tuple-element.4.field, f32[8,256]{1,0:T(8,128)S(1)} %get-tuple-element.5.gradient), custom_call_target="tpu_custom_call" | custom-call | tf_op jit(solution)/shard_map/pallas_call | solution.py:422
